TPU v7x, 32 devices: a whole 2x2x4 slice. The times are simulated.
32 devices in a mesh: key: 4 (over x, core), head: 4 (over z), batch: 2 (over y).
Axes of the slice: x: 2, y: 2, z: 4, core: 2. Of those that a mesh axis runs over, the one named last changes fastest.
Arguments:
- new_queries: bfloat16 [16, 4, 4, 1024], P('batch', 'head'), parts along dimension 0, may hold values from -6 to 6
- new_keys: bfloat16 [16, 4, 4, 1024], P('batch', 'head'), parts along dimension 0, may hold values from -0.8984375 to 0.8984375
- new_values: bfloat16 [16, 4, 4, 1024], P('batch', 'head'), parts along dimension 0, may hold values from -6 to 6
- decay_gate: float32 [16, 4, 4], P('batch', 'head'), parts along dimension 0, may hold values from 0.85 to 0.999
- write_gate: float32 [16, 4, 4], P('batch', 'head'), parts along dimension 0, may hold values from 0.2 to 1
- ridge_shift: float32 [4], P('head'), may hold values from 0.5 to 2
- norm_gain: float32 [4, 1024], P('head', 'key'), may hold values from 0.1 to 1.9
- cov_state: bfloat16 [16, 4, 1024, 1024], P('batch', 'head', 'key'), parts along dimension 0, may hold values from -1 to 42, as said below
- value_state: bfloat16 [16, 4, 1024, 1024], P('batch', 'head', None, 'key'), parts along dimension 0, may hold values from -0.1875 to 0.1875
- out_weight: bfloat16 [4, 1024, 8192], P('head', 'key'), may hold values from -0.125 to 0.125
Outputs:
- layer_out: bfloat16 [16, 4, 8192], P('batch', None, ('key', 'head')), parts along dimension 0
There are 2 independent parts, one for each index of `batch`. A program takes and returns all parts, laid end to end along the dimension named above; an argument that names none is the same for every part. Nothing has to cross between parts.
Inputs may be any that keep to these rules, and one draw needn't show every extreme that they name: `cov_state`: each 1024 x 1024 block is symmetric and positive definite.
All inputs are finite; a program needn't handle non-finite values.
Results may differ from a plain program's by a relative error of at most 0.0085.
Values may be sent and summed in bfloat16 or wider, within the bound.
A program may use at most 64 MiB of HBM per device.

v0:
```python
import jax
import jax.numpy as jnp
from jax import lax
from jax.sharding import PartitionSpec as P

DRAFT = 4
ITERS = 3


def coefficients(decay_gate, write_gate):
    decay_total = jnp.cumprod(decay_gate, axis=-1)
    decay_ratio = decay_total[..., :, None] / decay_total[..., None, :]
    is_later = jnp.arange(DRAFT)[:, None] >= jnp.arange(DRAFT)[None, :]
    mix_weights = jnp.where(
        is_later, write_gate[..., None, :] * decay_ratio, jnp.zeros_like(decay_ratio)
    )
    return (decay_total, mix_weights)


def body(
    new_queries,
    new_keys,
    new_values,
    decay_gate,
    write_gate,
    ridge_shift,
    norm_gain,
    cov_state,
    value_state,
    out_weight,
):
    high = lax.Precision.HIGHEST
    row_count = cov_state.shape[2]
    row_start = lax.axis_index("key") * row_count
    decay_total, mix_weights = coefficients(decay_gate, write_gate)
    ridge_term = ridge_shift[None, :, None, None]
    key_rows = lax.dynamic_slice_in_dim(new_keys, row_start, row_count, 3).astype(jnp.float32)
    residual = new_queries.astype(jnp.float32)
    direction = residual
    solution = jnp.zeros_like(residual)
    sq_norm = jnp.sum(residual * residual, axis=-1)
    for sweep_index in range(ITERS):
        dir_bf = direction.astype(jnp.bfloat16)
        dir_rows = lax.dynamic_slice_in_dim(direction, row_start, row_count, 3)
        state_prod = jnp.einsum(
            "shic,shtc->shti", cov_state, dir_bf, preferred_element_type=jnp.float32
        )
        key_dots = jnp.einsum(
            "shtc,shuc->shtu", dir_bf, new_keys, preferred_element_type=jnp.float32
        )
        low_rank = jnp.einsum("shtu,shuc->shtc", mix_weights * key_dots, key_rows, precision=high)
        applied = lax.all_gather(
            decay_total[..., None] * state_prod + low_rank + ridge_term * dir_rows,
            "key",
            axis=3,
            tiled=True,
        )
        step_size = sq_norm / jnp.sum(direction * applied, axis=-1)
        solution = solution + step_size[..., None] * direction
        residual = residual - step_size[..., None] * applied
        new_norm = jnp.sum(residual * residual, axis=-1)
        direction = residual + (new_norm / sq_norm)[..., None] * direction
        sq_norm = new_norm
    sol_rows = lax.dynamic_slice_in_dim(solution, row_start, row_count, 3)
    sol_bf = sol_rows.astype(jnp.bfloat16)
    state_read = jnp.einsum(
        "shvc,shtc->shtv", value_state, sol_bf, preferred_element_type=jnp.float32
    )
    key_sol = jnp.einsum("shtc,shuc->shtu", sol_bf.astype(jnp.float32), key_rows, precision=high)
    read_part = decay_total[..., None] * state_read + jnp.einsum(
        "shtu,shuv->shtv", mix_weights * key_sol, new_values.astype(jnp.float32), precision=high
    )
    value_count = value_state.shape[2]
    read_mine = lax.psum_scatter(read_part, "key", scatter_dimension=3, tiled=True)
    mean_sq = lax.psum(jnp.sum(read_mine * read_mine, axis=-1), "key") / value_count
    normed = (
        read_mine * lax.rsqrt(mean_sq + 1e-06)[..., None] * norm_gain[None, :, None, :]
    ).astype(jnp.bfloat16)
    partial_out = jnp.einsum(
        "shtv,hvm->stm", normed, out_weight, preferred_element_type=jnp.float32
    )
    summed = lax.psum_scatter(partial_out, ("key", "head"), scatter_dimension=2, tiled=True)
    return summed.astype(jnp.bfloat16)


def solution(mesh):
    placed = (
        P("batch", "head", None, None),
        P("batch", "head", None, None),
        P("batch", "head", None, None),
        P("batch", "head", None),
        P("batch", "head", None),
        P("head"),
        P("head", "key"),
        P("batch", "head", "key", None),
        P("batch", "head", None, "key"),
        P("head", "key", None),
    )
    return jax.shard_map(
        body,
        mesh=mesh,
        in_specs=placed,
        out_specs=P("batch", None, ("key", "head")),
        check_vma=False,
    )
```

profile of v0, /device:TPU:0, one launch (start us, length us, event | category | flops | bytes accessed | tf_op | source)
XLA Modules:
  0.0 147.2 jit_solution(12016023071875384271)
XLA Ops:
  6.5 0.0 copy-start
  6.5 0.0 copy-start.3
  6.5 0.0 copy-start.4
  6.5 0.0 reduce-scatter.7.cloned.1.call-start
  7.3 0.7 reduce_window.12
  8.0 0.1 copy.20
  8.1 0.8 copy.23
  8.8 0.8 bitcast_convert_fusion
  9.7 0.0 copy-start.1
  9.7 1.2 convolution_multiply_fusion.3
  10.9 1.0 fusion.73
  11.9 3.4 %fusion.47 = f32[8,1,4,256]{3,2,0,1:T(4,128)S(1)} fusion(f32[8,4,256]{2,1,0:T(4,128)S(1)} %fusion.73, bf16[8,1,256,1024]{3,2,1,0:T(8,128)(2,1)} %param.17, bf16[8,1,4,1024]{3,2,1,0:T(4,128)(2,1)} %param.10, f32[8,1,4,1024]{3,2,0,1:T(4,128)S(1)} %bitcast_convert_fusion, s32[]{:T(128)S(6)} %select_n.13, f32[]{:T(128)} %bitcast.125, f32[8,4]{1,0:T(8,128)S(1)} %copy.20), kind=kOutput, calls=%fused_computation.24 | convolution fusion | flops 16809984 | bytes 4358280 | tf_op jit(solution)/shard_map/shic,shtc->shti/dot_general | solution.py:45
  15.3 6.5 %all_gather.9 = f32[8,1,4,1024]{3,2,0,1:T(4,128)S(1)} all-gather(f32[8,1,4,256]{3,2,0,1:T(4,128)S(1)} %fusion.47), channel_id=1, replica_groups=mesh['key'=4,'head'=4,'batch'=2] {'key'}, dimensions={3}, use_global_device_ids=true | all-gather | bytes 163840 | tf_op jit(solution)/shard_map/all_gather | solution.py:52
  21.8 0.0 copy-done.3
  21.8 0.1 multiply_reduce_fusion.4
  22.0 0.2 multiply_reduce_fusion.3
  22.2 0.1 multiply_add_fusion.1
  22.3 0.0 copy-done.4
  22.3 0.2 convolution_multiply_fusion.2
  22.5 0.2 fusion.71
  22.7 0.0 copy-done.1
  22.7 1.2 fusion.44
  23.9 0.0 copy-start.2
  23.9 5.7 %all_gather.10 = f32[8,1,4,1024]{3,2,0,1:T(4,128)S(1)} all-gather(f32[8,1,4,256]{3,2,0,1:T(4,128)S(1)} %fusion.44), channel_id=1, replica_groups=mesh['key'=4,'head'=4,'batch'=2] {'key'}, dimensions={3}, use_global_device_ids=true | all-gather | bytes 163840 | tf_op jit(solution)/shard_map/all_gather | solution.py:52
  29.6 0.1 multiply_reduce_fusion.2
  29.7 0.2 multiply_reduce_fusion.1
  29.9 0.1 multiply_add_fusion
  30.1 0.2 convolution_multiply_fusion.1
  30.3 0.2 fusion.69
  30.5 1.2 fusion.41
  31.6 5.4 %all_gather.11 = f32[8,1,4,1024]{3,2,0,1:T(4,128)S(1)} all-gather(f32[8,1,4,256]{3,2,0,1:T(4,128)S(1)} %fusion.41), channel_id=1, replica_groups=mesh['key'=4,'head'=4,'batch'=2] {'key'}, dimensions={3}, use_global_device_ids=true | all-gather | bytes 163840 | tf_op jit(solution)/shard_map/all_gather | solution.py:52
  37.1 0.1 multiply_reduce_fusion
  37.2 0.1 add_convert_fusion
  37.3 0.1 convolution_multiply_fusion
  37.4 0.0 copy-done.2
  37.4 1.2 fusion.11
  38.6 0.0 copy-done
  38.6 0.3 fusion.10
  38.9 2.6 %copy.30 = f32[8,1,4,1024]{2,0,1,3:T(8,128)} copy(f32[8,1,4,1024]{3,2,0,1:T(4,128)S(1)} %fusion.10) | data formatting | bytes 262144
  41.5 0.0 copy-start.5
  41.5 3.9 %reshape.181 = f32[1024,32]{1,0:T(8,128)} reshape(f32[1024,1,8,4]{3,2,1,0:T(8,128)} %bitcast.128) | data formatting | bytes 262144
  45.5 0.0 reduce-scatter.7.cloned.1.call-update
  45.5 0.0 reduce-scatter.5.cloned.1.call-start
  45.6 23.2 %reduce-scatter.7.cloned.1.call-done = f32[256,32]{1,0:T(8,128)} async-done(((f32[1024,32]{1,0:T(8,128)}), f32[256,32]{1,0:T(8,128)}) %reduce-scatter.7.cloned.1.call-update) | async-done | bytes 32784
  68.8 1.2 reshape.182
  70.0 0.4 copy.31
  70.4 0.1 multiply_reduce_fusion.6
  70.5 0.1 copy.26
  70.5 5.7 %psum.7 = f32[8,1,4]{0,2,1:T(4,128)S(1)} all-reduce(f32[8,1,4]{0,2,1:T(4,128)S(1)} %bitcast.130), channel_id=1, replica_groups=mesh['key'=4,'head'=4,'batch'=2] {'key'}, use_global_device_ids=true, to_apply=%region_9.10 | all-reduce | flops 32 | bytes 256 | tf_op jit(solution)/shard_map/psum | solution.py:75
  76.3 0.1 copy.27
  76.4 0.0 copy-done.5
  76.4 0.1 fusion.65
  76.5 4.0 %fusion = f32[8,4,8192]{2,0,1:T(8,128)} fusion(bf16[1,256,8192]{2,1,0:T(8,128)(2,1)} %param.19, bf16[8,4,256]{2,1,0:T(4,128)(2,1)S(1)} %fusion.65), kind=kOutput, calls=%fused_computation | convolution fusion | flops 134217728 | bytes 5259264 | tf_op jit(solution)/shard_map/shtv,hvm->stm/dot_general | solution.py:79
  80.4 0.0 reduce-scatter.5.cloned.1.call-update
  80.5 58.4 %reduce-scatter.5.cloned.1.call-done = f32[8,4,512]{2,0,1:T(8,128)} async-done(((f32[8,4,8192]{2,0,1:T(8,128)}), f32[8,4,512]{2,0,1:T(8,128)}) %reduce-scatter.5.cloned.1.call-update) | async-done | bytes 65552 | tf_op jit(solution)/shard_map/reduce_scatter | solution.py:82
  138.9 0.8 convert_element_type.27
  139.8 0.6 copy.29
  (7 shorter events, 0.1 us)
Async XLA Ops:
  6.5 32.1 %copy-start = (bf16[8,1,4,1024]{3,2,1,0:T(4,128)(2,1)S(1)}, bf16[8,1,4,1024]{3,2,1,0:T(4,128)(2,1)}, u32[]{:S(2)}) copy-start(bf16[8,1,4,1024]{3,2,1,0:T(4,128)(2,1)} %param.12) | copy-start | bytes 196612
  6.5 15.3 %copy-start.3 = (bf16[8,1,4,1024]{3,2,1,0:T(4,128)(2,1)S(1)}, bf16[8,1,4,1024]{3,2,1,0:T(4,128)(2,1)}, u32[]{:S(2)}) copy-start(bf16[8,1,4,1024]{3,2,1,0:T(4,128)(2,1)} %param.10) | copy-start | bytes 196612
  6.5 15.8 %copy-start.4 = (bf16[8,1,4,1024]{3,2,1,0:T(4,128)(2,1)S(1)}, bf16[8,1,4,1024]{3,2,1,0:T(4,128)(2,1)}, u32[]{:S(2)}) copy-start(bf16[8,1,4,1024]{3,2,1,0:T(4,128)(2,1)} %param.11) | copy-start | bytes 196612
  6.5 62.2 %reduce-scatter.7.cloned.1.call-start = ((), (), s32[]{:S(2)}) async-start(), calls=%async_computation.3 | async-start | bytes 655360
  9.7 13.0 %copy-start.1 = (bf16[8,1,256,1024]{3,2,1,0:T(8,128)(2,1)S(1)}, bf16[8,1,256,1024]{3,2,1,0:T(8,128)(2,1)}, u32[]{:S(2)}) copy-start(bf16[8,1,256,1024]{3,2,1,0:T(8,128)(2,1)} %param.17) | copy-start | bytes 12582916
  23.9 13.6 %copy-start.2 = (bf16[8,1,1024,256]{3,2,1,0:T(8,128)(2,1)S(1)}, bf16[8,1,1024,256]{3,2,1,0:T(8,128)(2,1)}, u32[]{:S(2)}) copy-start(bf16[8,1,1024,256]{3,2,1,0:T(8,128)(2,1)} %param.18) | copy-start | bytes 12582916
  41.5 34.8 %copy-start.5 = (f32[1,256]{1,0:T(1,128)S(1)}, f32[1,256]{1,0:T(1,128)}, u32[]{:S(2)}) copy-start(f32[1,256]{1,0:T(1,128)} %param.16) | copy-start | bytes 3076
  45.5 93.4 %reduce-scatter.5.cloned.1.call-start = ((), (), s32[]{:S(2)}) async-start(), calls=%async_computation.2 | async-start | bytes 1114112 | tf_op jit(solution)/shard_map/reduce_scatter | solution.py:82
Sparse Core Ops, SparseCore 0:
  45.6 23.0 reduce-scatter.6
  80.6 58.2 reduce-scatter.4
where the time goes:
time: 148 us; the launch traced here: 147 us
  waiting for transfers between devices  81.7 us (55%)
  blocking collectives  23.4 us (16%)
  matrix products  14.3 us (10%)
  between operations  14.2 us (10%)
  local copies, waits for them, and re-layouts  9.86 us (7%)
  other arithmetic  3.79 us (3%)
    reduce_scatter x1, waiting for transfers between devices, body(): lax.psum_scatter(partial_out, ('key', 'head'), scatter_dimension=2, tiled...  58.4 us
    unnamed x3, waiting for transfers between devices  23.2 us
    all_gather x3, blocking collectives, body(): lax.all_gather(decay_total[..., None] * state_prod + low_rank + ridge_ter...  17.7 us
    unnamed x16, local copies, waits for them, and re-layouts  8.22 us
    dot_general x3, matrix products, body(): jnp.einsum('shic,shtc->shti', cov_state, dir_bf, preferred_element_type=j...  5.8 us
    psum x1, blocking collectives, body(): lax.psum(jnp.sum(read_mine * read_mine, axis=-1), 'key') / value_count  5.73 us
    dot_general x1, matrix products, body(): jnp.einsum('shtv,hvm->stm', normed, out_weight, preferred_element_type=jn...  3.98 us
  transfers between devices with their start and end apart: 2, of which 2 were waited for; matrix products, arithmetic and copies ran while one was open for 0% of the time, Pallas kernels for 0%

commit v1 on v0

v1 whole, which is shorter than its diff:
```python
import functools

import jax
import jax.numpy as jnp
from jax import lax
from jax.experimental import pallas as pl
from jax.experimental.pallas import tpu as pltpu
from jax.sharding import PartitionSpec as P

ITERS = 3
MESH = pl.DeviceIdType.MESH
F32 = jnp.float32
BF16 = jnp.bfloat16
HIGH = lax.Precision.HIGHEST
GROUP = 16


def dot_nt(a, b):
    return lax.dot_general(a, b, (((1,), (1,)), ((), ())), preferred_element_type=F32)


def dot_high(a, b):
    return lax.dot_general(
        a, b, (((1,), (0,)), ((), ())), precision=HIGH, preferred_element_type=F32
    )


def kernel(
    n_key,
    n_head,
    q_h,
    k_h,
    v_h,
    dg_h,
    wg_h,
    ridge_ref,
    gain_h,
    cov_h,
    vs_h,
    w_h,
    out_ref,
    q_v,
    k_v,
    v_v,
    dg_v,
    wg_v,
    gain_v,
    cov_v,
    vs_v,
    w_v,
    dgx,
    wgx,
    kf,
    vf,
    dref,
    rref,
    xref,
    bref,
    img,
    rd_send,
    rd_recv,
    den_send,
    den_recv,
    sq_send,
    sq_recv,
    core_send,
    core_recv,
    own,
    x_send,
    x_recv,
    keep,
    z_send,
    z_recv,
    in_sem,
    cov_sem,
    vs_sem,
    w_sem,
    img_ss,
    img_rs,
    rd_ss,
    rd_rs,
    den_ss,
    den_rs,
    sq_ss,
    sq_rs,
    core_ss,
    core_rs,
    x_ss,
    x_rs,
    z_ss,
    z_rs,
):
    key = lax.axis_index("key")
    head = lax.axis_index("head")
    seqs, draft, width = q_v.shape
    rows = cov_v.shape[1]
    values = vs_v.shape[1]
    vcols = values // n_key
    n = seqs * draft
    block = out_ref.shape[1]
    per_group = GROUP // draft

    barrier = pltpu.get_barrier_semaphore()
    for d in range(1, n_key):
        pl.semaphore_signal(
            barrier, inc=1, device_id={"key": lax.rem(key + d, n_key)}, device_id_type=MESH
        )
    for d in range(1, n_head):
        pl.semaphore_signal(
            barrier, inc=1, device_id={"head": lax.rem(head + d, n_head)}, device_id_type=MESH
        )

    small = []
    pairs = ((q_h.at[:, 0], q_v), (k_h.at[:, 0], k_v), (dg_h, dg_v), (wg_h, wg_v), (v_h.at[:, 0], v_v), (gain_h, gain_v))
    for i, (src, dst) in enumerate(pairs):
        small.append(pltpu.make_async_copy(src, dst, in_sem.at[i]))
    cov_in = [pltpu.make_async_copy(cov_h.at[s, 0], cov_v.at[s], cov_sem.at[s]) for s in range(seqs)]
    vs_in = [pltpu.make_async_copy(vs_h.at[s, 0], vs_v.at[s], vs_sem.at[s]) for s in range(seqs)]
    w_in = pltpu.make_async_copy(w_h.at[0], w_v, w_sem)
    for c in small + cov_in + vs_in + [w_in]:
        c.start()
    for c in small:
        c.wait()

    for s in range(seqs):
        at = pl.ds(s * draft, draft)
        dref[at, :] = q_v[s].astype(F32)
        kf[at, :] = k_v[s].astype(F32)
        vf[at, :] = v_v[s].astype(F32)
        dgx[at, :] = jnp.broadcast_to(dg_v[s], (draft, draft))
        wgx[at, :] = jnp.broadcast_to(wg_v[s], (draft, draft))

    row_id = lax.broadcasted_iota(jnp.int32, (n, 1), 0)
    tok = lax.rem(row_id, draft)
    first = row_id - tok
    gates, writes = dgx[...], wgx[...]
    totals = [gates[:, 0:1]]
    for u in range(1, draft):
        totals.append(totals[-1] * gates[:, u : u + 1])
    decay = totals[0]
    for u in range(1, draft):
        decay = jnp.where(tok == u, totals[u], decay)
    col_id = lax.broadcasted_iota(jnp.int32, (n, n), 1)
    mix = jnp.zeros((n, n), F32)
    for u in range(draft):
        weight = writes[:, u : u + 1] * (decay / totals[u])
        mix = jnp.where((col_id == first + u) & (tok >= u), weight, mix)
    lane = lax.broadcasted_iota(jnp.int32, (n, 128), 1)
    diag = lane == lax.broadcasted_iota(jnp.int32, (n, 128), 0)

    def as_row(column):
        row = jnp.sum(jnp.where(diag, column, 0.0), axis=0, keepdims=True)
        return jnp.broadcast_to(row, (8, 128))

    def as_column(row):
        return jnp.sum(jnp.where(diag, row[0:1, :], 0.0), axis=1, keepdims=True)

    ridge = ridge_ref[0]
    keys = kf[...]
    keys_b = keys.astype(BF16)
    group_row = lax.broadcasted_iota(jnp.int32, (GROUP, 1), 0) // draft

    def local_product(dir_b, wait):
        parts = []
        for g in range(n // GROUP):
            lhs = dir_b[g * GROUP : (g + 1) * GROUP]
            acc = None
            for j in range(per_group):
                s = g * per_group + j
                if wait:
                    cov_in[s].wait()
                prod = dot_nt(lhs, cov_v[s])
                acc = prod if acc is None else jnp.where(group_row == j, prod, acc)
            parts.append(acc)
        return decay * jnp.concatenate(parts, axis=0)

    mine = pl.ds(pl.multiple_of(key * rows, 128), rows)
    direction = dref[...]
    rref[...] = direction
    sq_norm = jnp.sum(direction * direction, axis=1, keepdims=True)
    sends = []
    for it in range(ITERS - 1):
        dir_b = dref[...].astype(BF16)
        img[it, key] = local_product(dir_b, it == 0)
        if it == 0:
            pl.semaphore_wait(barrier, n_key - 1 + n_head - 1)
        copies = []
        for d in range(1, n_key):
            c = pltpu.make_async_remote_copy(
                src_ref=img.at[it, key],
                dst_ref=img.at[it, key],
                send_sem=img_ss.at[it, d],
                recv_sem=img_rs.at[it, d],
                device_id={"key": lax.rem(key + d, n_key)},
                device_id_type=MESH,
            )
            c.start()
            copies.append(c)
        dots = dot_nt(dir_b, keys_b)
        bref[...] = dot_high(mix * dots, keys) + ridge * dref[...]
        for c in copies:
            c.wait_recv()
        sends += copies
        applied = jnp.concatenate([img[it, j] for j in range(n_key)], axis=1) + bref[...]
        direction = dref[...]
        step = sq_norm / jnp.sum(direction * applied, axis=1, keepdims=True)
        if it == 0:
            xref[...] = step * direction
        else:
            xref[...] = xref[...] + step * direction
        residual = rref[...] - step * applied
        rref[...] = residual
        new_norm = jnp.sum(residual * residual, axis=1, keepdims=True)
        dref[...] = residual + (new_norm / sq_norm) * direction
        sq_norm = new_norm

    dir_b = dref[...].astype(BF16)
    image = local_product(dir_b, False)
    den_send[...] = as_row(jnp.sum(image * dref[:, mine], axis=1, keepdims=True))
    for d in range(1, n_key):
        c = pltpu.make_async_remote_copy(
            src_ref=den_send,
            dst_ref=den_recv.at[d],
            send_sem=den_ss.at[d],
            recv_sem=den_rs.at[d],
            device_id={"key": lax.rem(key + d, n_key)},
            device_id_type=MESH,
        )
        c.start()
        sends.append(c)
    dens = sends[-(n_key - 1) :]

    x_rows = xref[:, mine].astype(BF16)
    d_rows = dref[:, mine].astype(BF16)
    for g in range(n // GROUP):
        at = slice(g * GROUP, (g + 1) * GROUP)
        lhs = jnp.concatenate([x_rows[at], d_rows[at]], axis=0)
        acc_x = acc_d = None
        for j in range(per_group):
            s = g * per_group + j
            vs_in[s].wait()
            prod = dot_nt(lhs, vs_v[s])
            px, pd = prod[:GROUP], prod[GROUP:]
            acc_x = px if acc_x is None else jnp.where(group_row == j, px, acc_x)
            acc_d = pd if acc_d is None else jnp.where(group_row == j, pd, acc_d)
        acc_x = (decay[at] * acc_x).astype(BF16)
        acc_d = (decay[at] * acc_d).astype(BF16)
        for j in range(n_key):
            cols = slice(j * vcols, (j + 1) * vcols)
            rd_send[j, 0, at, :] = acc_x[:, cols]
            rd_send[j, 1, at, :] = acc_d[:, cols]
    reads = []
    for d in range(1, n_key):
        to = lax.rem(key + d, n_key)
        c = pltpu.make_async_remote_copy(
            src_ref=rd_send.at[to],
            dst_ref=rd_recv.at[d],
            send_sem=rd_ss.at[d],
            recv_sem=rd_rs.at[d],
            device_id={"key": to},
            device_id_type=MESH,
        )
        c.start()
        reads.append(c)
    sends += reads
    dots_d = dot_nt(dir_b, keys_b)
    dots_x = dot_nt(xref[...].astype(BF16), keys_b)
    base = dot_high(mix * dots_d, keys) + ridge * dref[...]
    den = jnp.sum(base * dref[...], axis=1, keepdims=True) + as_column(den_send[...])
    vcol = pl.ds(pl.multiple_of(key * vcols, 128), vcols)
    vals = vf[:, vcol]
    read_x = dot_high(mix * dots_x, vals) + rd_send[key, 0].astype(F32)
    read_d = dot_high(mix * dots_d, vals) + rd_send[key, 1].astype(F32)
    for d in range(1, n_key):
        dens[d - 1].wait_recv()
        den = den + as_column(den_recv[d])
    step = sq_norm / den
    for d in range(1, n_key):
        reads[d - 1].wait_recv()
        read_x = read_x + rd_recv[d, 0].astype(F32)
        read_d = read_d + rd_recv[d, 1].astype(F32)
    read = read_x + step * read_d

    sq_send[...] = as_row(jnp.sum(read * read, axis=1, keepdims=True))
    squares = []
    for d in range(1, n_key):
        c = pltpu.make_async_remote_copy(
            src_ref=sq_send,
            dst_ref=sq_recv.at[d],
            send_sem=sq_ss.at[d],
            recv_sem=sq_rs.at[d],
            device_id={"key": lax.rem(key + d, n_key)},
            device_id_type=MESH,
        )
        c.start()
        squares.append(c)
    sends += squares
    gained = (read * gain_v[...]).astype(BF16)
    w_in.wait()

    core = lax.rem(key, 2)
    chip = key // 2
    partner = key + 1 - 2 * core
    across = lax.rem(key + 2, n_key)

    def project(to_key, to_head):
        at = pl.multiple_of((to_key * n_head + to_head) * block, 128)
        return jnp.dot(gained, w_v[:, pl.ds(at, block)], preferred_element_type=F32)

    order = list(range(1, n_head)) + [0]
    core_copy, x_copy, z_copy = {}, {}, {}
    scale = []

    def stage_a(o):
        to = lax.rem(head + o, n_head)
        for half in range(2):
            core_send[o, half] = project(2 * half + 1 - core, to).astype(BF16)
        c = pltpu.make_async_remote_copy(
            src_ref=core_send.at[o],
            dst_ref=core_recv.at[o],
            send_sem=core_ss.at[o],
            recv_sem=core_rs.at[o],
            device_id={"key": partner},
            device_id_type=MESH,
        )
        c.start()
        core_copy[o] = c
        for half in range(2):
            own[o, half] = project(2 * half + core, to)

    def stage_b(o):
        core_copy[o].wait_recv()
        other = 1 - chip
        x_send[o] = (own[o, other] + core_recv[o, other].astype(F32)).astype(BF16)
        c = pltpu.make_async_remote_copy(
            src_ref=x_send.at[o],
            dst_ref=x_recv.at[o],
            send_sem=x_ss.at[o],
            recv_sem=x_rs.at[o],
            device_id={"key": across},
            device_id_type=MESH,
        )
        c.start()
        x_copy[o] = c
        keep[o] = own[o, chip] + core_recv[o, chip].astype(F32)

    def stage_c(o):
        if not scale:
            total = as_column(sq_send[...])
            for d in range(1, n_key):
                squares[d - 1].wait_recv()
                total = total + as_column(sq_recv[d])
            scale.append(lax.rsqrt(total / values + 1e-06))
        x_copy[o].wait_recv()
        done = (keep[o] + x_recv[o].astype(F32)) * scale[0]
        if o == 0:
            keep[o] = done
            return
        z_send[o] = done.astype(BF16)
        c = pltpu.make_async_remote_copy(
            src_ref=z_send.at[o],
            dst_ref=z_recv.at[o],
            send_sem=z_ss.at[o],
            recv_sem=z_rs.at[o],
            device_id={"head": lax.rem(head + o, n_head)},
            device_id_type=MESH,
        )
        c.start()
        z_copy[o] = c

    for i in range(n_head + 2):
        if i < n_head:
            stage_a(order[i])
        if 0 <= i - 1 < n_head:
            stage_b(order[i - 1])
        if 0 <= i - 2 < n_head:
            stage_c(order[i - 2])
    result = keep[0]
    for o in range(1, n_head):
        z_copy[o].wait_recv()
        result = result + z_recv[o].astype(F32)
    out_ref[...] = result
    for c in sends + list(core_copy.values()) + list(x_copy.values()) + list(z_copy.values()):
        c.wait_send()


def solution(mesh):
    n_key, n_head = mesh.shape["key"], mesh.shape["head"]
    assert n_key == 4

    def body(q, k, v, dg, wg, ridge, gain, cov, vs, w):
        seqs, _, draft, width = q.shape
        rows = cov.shape[2]
        values = vs.shape[2]
        vcols = values // n_key
        model = w.shape[2]
        block = model // (n_key * n_head)
        n = seqs * draft
        dma = pltpu.SemaphoreType.DMA
        out = pl.pallas_call(
            functools.partial(kernel, n_key, n_head),
            out_shape=jax.ShapeDtypeStruct((n, block), F32),
            in_specs=[pl.BlockSpec(memory_space=pl.ANY)] * 5
            + [pl.BlockSpec(memory_space=pltpu.SMEM)]
            + [pl.BlockSpec(memory_space=pl.ANY)] * 4,
            out_specs=pl.BlockSpec(memory_space=pltpu.VMEM),
            scratch_shapes=[
                pltpu.VMEM((seqs, draft, width), BF16),
                pltpu.VMEM((seqs, draft, width), BF16),
                pltpu.VMEM((seqs, draft, values), BF16),
                pltpu.VMEM(dg.shape, F32),
                pltpu.VMEM(wg.shape, F32),
                pltpu.VMEM(gain.shape, F32),
                pltpu.VMEM((seqs, rows, width), BF16),
                pltpu.VMEM((seqs, values, rows), BF16),
                pltpu.VMEM(w.shape[1:], BF16),
                pltpu.VMEM((n, draft), F32),
                pltpu.VMEM((n, draft), F32),
                pltpu.VMEM((n, width), F32),
                pltpu.VMEM((n, values), F32),
                pltpu.VMEM((n, width), F32),
                pltpu.VMEM((n, width), F32),
                pltpu.VMEM((n, width), F32),
                pltpu.VMEM((n, width), F32),
                pltpu.VMEM((ITERS - 1, n_key, n, rows), F32),
                pltpu.VMEM((n_key, 2, n, vcols), BF16),
                pltpu.VMEM((n_key, 2, n, vcols), BF16),
                pltpu.VMEM((8, 128), F32),
                pltpu.VMEM((n_key, 8, 128), F32),
                pltpu.VMEM((8, 128), F32),
                pltpu.VMEM((n_key, 8, 128), F32),
                pltpu.VMEM((n_head, 2, n, block), BF16),
                pltpu.VMEM((n_head, 2, n, block), BF16),
                pltpu.VMEM((n_head, 2, n, block), F32),
                pltpu.VMEM((n_head, n, block), BF16),
                pltpu.VMEM((n_head, n, block), BF16),
                pltpu.VMEM((n_head, n, block), F32),
                pltpu.VMEM((n_head, n, block), BF16),
                pltpu.VMEM((n_head, n, block), BF16),
                dma((6,)),
                dma((seqs,)),
                dma((seqs,)),
                dma,
                dma((ITERS - 1, n_key)),
                dma((ITERS - 1, n_key)),
                dma((n_key,)),
                dma((n_key,)),
                dma((n_key,)),
                dma((n_key,)),
                dma((n_key,)),
                dma((n_key,)),
                dma((n_head,)),
                dma((n_head,)),
                dma((n_head,)),
                dma((n_head,)),
                dma((n_head,)),
                dma((n_head,)),
            ],
            compiler_params=pltpu.CompilerParams(collective_id=0, has_side_effects=True),
        )(q, k, v, dg, wg, ridge, gain, cov, vs, w)
        return out.astype(BF16).reshape(seqs, draft, block)

    placed = (
        P("batch", "head", None, None),
        P("batch", "head", None, None),
        P("batch", "head", None, None),
        P("batch", "head", None),
        P("batch", "head", None),
        P("head"),
        P("head", "key"),
        P("batch", "head", "key", None),
        P("batch", "head", None, "key"),
        P("head", "key", None),
    )
    return jax.shard_map(
        body,
        mesh=mesh,
        in_specs=placed,
        out_specs=P("batch", None, ("key", "head")),
        check_vma=False,
    )
```

time: 148 us -> 40.2 us (0.27)
  waiting for transfers between devices: 81.7 us -> 0 us
  Pallas kernels: 0 us -> 35.2 us
  blocking collectives: 23.4 us -> 0 us
  matrix products: 14.3 us -> 0 us
  between operations: 14.2 us -> 0.66 us
  local copies, waits for them, and re-layouts: 9.86 us -> 3.32 us
  other arithmetic: 3.79 us -> 0.85 us
    reduce_scatter x1 -> x0, waiting for transfers between devices: 58.4 us -> none  [body(): lax.psum_scatter(partial_out, ('key', 'head'), scatter_dimension=2, tiled...]
    pallas_call x0 -> x1, Pallas kernels: none -> 35.2 us  [body(): pl.pallas_call(functools.partial(kernel, n_key, n_head), out_shape=jax.Sh...]
    unnamed x3 -> x0, waiting for transfers between devices: 23.2 us -> none
    all_gather x3 -> x0, blocking collectives: 17.7 us -> none  [body(): lax.all_gather(decay_total[..., None] * state_prod + low_rank + ridge_ter...]
    dot_general x13 -> x0, matrix products: 14.3 us -> none  [the longest x3 5.8 us: body(): jnp.einsum('shic,shtc->shti', cov_state, dir_bf, preferred_element_type=j...]
    psum x1 -> x0, blocking collectives: 5.73 us -> none  [body(): lax.psum(jnp.sum(read_mine * read_mine, axis=-1), 'key') / value_count]
    unnamed x16 -> x2, local copies, waits for them, and re-layouts: 8.22 us -> 2.69 us
  transfers between devices with their start and end apart: 2 -> 0, of which waited for: 2 -> 0; matrix products, arithmetic and copies ran while one was open for 0% -> 0% of each run, Pallas kernels for 0% -> 0%
where the time goes in v1:
time: 40.2 us; the launch traced here: 40 us
  Pallas kernels  35.2 us (88%)
  local copies, waits for them, and re-layouts  3.32 us (8%)
  other arithmetic  0.85 us (2%)
  between operations  0.66 us (2%)
    pallas_call x1, Pallas kernels, body(): pl.pallas_call(functools.partial(kernel, n_key, n_head), out_shape=jax.Sh...  35.2 us
    unnamed x2, local copies, waits for them, and re-layouts  2.69 us
    convert_element_type x1, other arithmetic, body(): return out.astype(BF16).reshape(seqs, draft, block)  0.85 us

profile of v1, /device:TPU:0, one launch (start us, length us, event | category | flops | bytes accessed | tf_op | source)
XLA Modules:
  0.0 40.0 jit_solution(6002853485559230353)
XLA Ops:
  0.7 1.3 %copy.11.dg_h = f32[8,1,4]{2,1,0:T(1,128)} copy(f32[8,1,4]{0,2,1:T(4,128)} %param.13) | data formatting | bytes 256 | tf_op args[3]
  2.0 1.3 %copy.12.wg_h = f32[8,1,4]{2,1,0:T(1,128)} copy(f32[8,1,4]{0,2,1:T(4,128)} %param.14) | data formatting | bytes 256 | tf_op args[4]
  3.3 35.2 %shard_map.100 = f32[32,512]{1,0:T(8,128)} custom-call(bf16[8,1,4,1024]{3,2,1,0:T(4,128)(2,1)} %q_h.1, bf16[8,1,4,1024]{3,2,1,0:T(4,128)(2,1)} %k_h.1, bf16[8,1,4,1024]{3,2,1,0:T(4,128)(2,1)} %v_h.1, f32[8,1,4]{2,1,0:T(1,128)} %copy.11.dg_h, f32[8,1,4]{2,1,0:T(1,128)} %copy.12.wg_h, f32[1]{0:T(128)S(6)} %copy.13.ridge_ref, f32[1,256]{1,0:T(1,128)} %gain_h.1, ...), custom_call_target="tpu_custom_call" | custom-call | tf_op jit(solution)/shard_map/pallas_call | solution.py:400
  38.5 0.8 %convert_element_type.3 = bf16[32,512]{1,0:T(8,128)(2,1)S(1)} convert(f32[32,512]{1,0:T(8,128)} %shard_map.100) | non-fusion elementwise | flops 16384 | bytes 98304 | tf_op jit(solution)/shard_map/convert_element_type | solution.py:461
  39.4 0.6 %reshape.3 = bf16[8,4,512]{2,1,0:T(4,128)(2,1)} reshape(bf16[32,512]{1,0:T(8,128)(2,1)S(1)} %convert_element_type.3) | data formatting | bytes 65536 | tf_op jit(solution)/shard_map/reshape | solution.py:461

commit v2 on v1

--- a/solution.py
+++ b/solution.py
@@ -48,8 +48,6 @@
     cov_v,
     vs_v,
     w_v,
-    dgx,
-    wgx,
     kf,
     vf,
     dref,
@@ -97,7 +95,7 @@
     values = vs_v.shape[1]
     vcols = values // n_key
     n = seqs * draft
-    block = out_ref.shape[1]
+    block = out_ref.shape[2]
     per_group = GROUP // draft
 
     barrier = pltpu.get_barrier_semaphore()
@@ -127,23 +125,26 @@
         dref[at, :] = q_v[s].astype(F32)
         kf[at, :] = k_v[s].astype(F32)
         vf[at, :] = v_v[s].astype(F32)
-        dgx[at, :] = jnp.broadcast_to(dg_v[s], (draft, draft))
-        wgx[at, :] = jnp.broadcast_to(wg_v[s], (draft, draft))
 
     row_id = lax.broadcasted_iota(jnp.int32, (n, 1), 0)
     tok = lax.rem(row_id, draft)
     first = row_id - tok
-    gates, writes = dgx[...], wgx[...]
-    totals = [gates[:, 0:1]]
+    seq_hot = lax.broadcasted_iota(jnp.int32, (n, seqs), 1) == row_id // draft
+
+    def per_row(gates, u):
+        return jnp.sum(jnp.where(seq_hot, gates[u : u + 1, :], 0.0), axis=1, keepdims=True)
+
+    gates, writes = dg_v[0], wg_v[0]
+    totals = [per_row(gates, 0)]
     for u in range(1, draft):
-        totals.append(totals[-1] * gates[:, u : u + 1])
+        totals.append(totals[-1] * per_row(gates, u))
     decay = totals[0]
     for u in range(1, draft):
         decay = jnp.where(tok == u, totals[u], decay)
     col_id = lax.broadcasted_iota(jnp.int32, (n, n), 1)
     mix = jnp.zeros((n, n), F32)
     for u in range(draft):
-        weight = writes[:, u : u + 1] * (decay / totals[u])
+        weight = per_row(writes, u) * (decay / totals[u])
         mix = jnp.where((col_id == first + u) & (tok >= u), weight, mix)
     lane = lax.broadcasted_iota(jnp.int32, (n, 128), 1)
     diag = lane == lax.broadcasted_iota(jnp.int32, (n, 128), 0)
@@ -379,7 +380,9 @@
     for o in range(1, n_head):
         z_copy[o].wait_recv()
         result = result + z_recv[o].astype(F32)
-    out_ref[...] = result
+    keep[0] = result
+    for s in range(seqs):
+        out_ref[s] = keep[0, s * draft : (s + 1) * draft, :].astype(BF16)
     for c in sends + list(core_copy.values()) + list(x_copy.values()) + list(z_copy.values()):
         c.wait_send()
 
@@ -399,7 +402,7 @@
         dma = pltpu.SemaphoreType.DMA
         out = pl.pallas_call(
             functools.partial(kernel, n_key, n_head),
-            out_shape=jax.ShapeDtypeStruct((n, block), F32),
+            out_shape=jax.ShapeDtypeStruct((seqs, draft, block), BF16),
             in_specs=[pl.BlockSpec(memory_space=pl.ANY)] * 5
             + [pl.BlockSpec(memory_space=pltpu.SMEM)]
             + [pl.BlockSpec(memory_space=pl.ANY)] * 4,
@@ -408,14 +411,12 @@
                 pltpu.VMEM((seqs, draft, width), BF16),
                 pltpu.VMEM((seqs, draft, width), BF16),
                 pltpu.VMEM((seqs, draft, values), BF16),
-                pltpu.VMEM(dg.shape, F32),
-                pltpu.VMEM(wg.shape, F32),
+                pltpu.VMEM((1, draft, seqs), F32),
+                pltpu.VMEM((1, draft, seqs), F32),
                 pltpu.VMEM(gain.shape, F32),
                 pltpu.VMEM((seqs, rows, width), BF16),
                 pltpu.VMEM((seqs, values, rows), BF16),
                 pltpu.VMEM(w.shape[1:], BF16),
-                pltpu.VMEM((n, draft), F32),
-                pltpu.VMEM((n, draft), F32),
                 pltpu.VMEM((n, width), F32),
                 pltpu.VMEM((n, values), F32),
                 pltpu.VMEM((n, width), F32),
@@ -457,8 +458,19 @@
                 dma((n_head,)),
             ],
             compiler_params=pltpu.CompilerParams(collective_id=0, has_side_effects=True),
-        )(q, k, v, dg, wg, ridge, gain, cov, vs, w)
-        return out.astype(BF16).reshape(seqs, draft, block)
+        )(
+            q,
+            k,
+            v,
+            dg.transpose(1, 2, 0),
+            wg.transpose(1, 2, 0),
+            ridge,
+            gain,
+            cov,
+            vs,
+            w,
+        )
+        return out
 
     placed = (
         P("batch", "head", None, None),

time: 40.2 us -> 37.4 us (0.930)
  local copies, waits for them, and re-layouts: 3.32 us -> 1.39 us
  other arithmetic: 0.85 us -> 0 us
    unnamed x2 -> x1, local copies, waits for them, and re-layouts: 2.69 us -> 1.39 us
    convert_element_type x1 -> x0, other arithmetic: 0.85 us -> none  [body(): return out.astype(BF16).reshape(seqs, draft, block)]
    reshape x1 -> x0, local copies, waits for them, and re-layouts: 0.63 us -> none  [body(): return out.astype(BF16).reshape(seqs, draft, block)]
where the time goes in v2:
time: 37.4 us; the launch traced here: 37.2 us
  Pallas kernels  35.1 us (94%)
  local copies, waits for them, and re-layouts  1.39 us (4%)
  between operations  0.66 us (2%)
    pallas_call x1, Pallas kernels, body(): pl.pallas_call(functools.partial(kernel, n_key, n_head), out_shape=jax.Sh...  35.1 us
    unnamed x1, local copies, waits for them, and re-layouts  1.39 us

profile of v2, /device:TPU:0, one launch (start us, length us, event | category | flops | bytes accessed | tf_op | source)
XLA Modules:
  0.0 37.2 jit_solution(16106214707349574006)
XLA Ops:
  0.7 35.1 %shard_map.100 = bf16[8,4,512]{2,1,0:T(4,128)(2,1)} custom-call(bf16[8,1,4,1024]{3,2,1,0:T(4,128)(2,1)} %q_h.1, bf16[8,1,4,1024]{3,2,1,0:T(4,128)(2,1)} %k_h.1, bf16[8,1,4,1024]{3,2,1,0:T(4,128)(2,1)} %v_h.1, f32[1,4,8]{2,1,0:T(4,128)} %bitcast.2, f32[1,4,8]{2,1,0:T(4,128)} %bitcast.3, f32[1]{0:T(128)S(6)} %copy.12.ridge_ref, f32[1,256]{1,0:T(1,128)} %gain_h.1, ...), custom_call_target="tpu_custom_call" | custom-call | tf_op jit(solution)/shard_map/pallas_call | solution.py:403
  35.8 1.4 %copy.13 = bf16[8,4,512]{2,1,0:T(4,128)(2,1)} copy(bf16[8,4,512]{2,1,0:T(4,128)(2,1)} %shard_map.100) | data formatting | bytes 65536

commit v3 on v2

--- a/solution.py
+++ b/solution.py
@@ -115,7 +115,7 @@
     cov_in = [pltpu.make_async_copy(cov_h.at[s, 0], cov_v.at[s], cov_sem.at[s]) for s in range(seqs)]
     vs_in = [pltpu.make_async_copy(vs_h.at[s, 0], vs_v.at[s], vs_sem.at[s]) for s in range(seqs)]
     w_in = pltpu.make_async_copy(w_h.at[0], w_v, w_sem)
-    for c in small + cov_in + vs_in + [w_in]:
+    for c in small + cov_in:
         c.start()
     for c in small:
         c.wait()
@@ -161,19 +161,18 @@
     keys_b = keys.astype(BF16)
     group_row = lax.broadcasted_iota(jnp.int32, (GROUP, 1), 0) // draft
 
-    def local_product(dir_b, wait):
-        parts = []
-        for g in range(n // GROUP):
-            lhs = dir_b[g * GROUP : (g + 1) * GROUP]
-            acc = None
-            for j in range(per_group):
-                s = g * per_group + j
-                if wait:
-                    cov_in[s].wait()
-                prod = dot_nt(lhs, cov_v[s])
-                acc = prod if acc is None else jnp.where(group_row == j, prod, acc)
-            parts.append(acc)
-        return decay * jnp.concatenate(parts, axis=0)
+    groups = n // GROUP
+
+    def group_product(dir_b, g, wait):
+        lhs = dir_b[g * GROUP : (g + 1) * GROUP]
+        acc = None
+        for j in range(per_group):
+            s = g * per_group + j
+            if wait:
+                cov_in[s].wait()
+            prod = dot_nt(lhs, cov_v[s])
+            acc = prod if acc is None else jnp.where(group_row == j, prod, acc)
+        return decay[g * GROUP : (g + 1) * GROUP] * acc
 
     mine = pl.ds(pl.multiple_of(key * rows, 128), rows)
     direction = dref[...]
@@ -182,27 +181,32 @@
     sends = []
     for it in range(ITERS - 1):
         dir_b = dref[...].astype(BF16)
-        img[it, key] = local_product(dir_b, it == 0)
+        copies = []
+        for g in range(groups):
+            at = pl.ds(g * GROUP, GROUP)
+            img[it, key, at, :] = group_product(dir_b, g, it == 0).astype(BF16)
+            if it == 0 and g == 0:
+                pl.semaphore_wait(barrier, n_key - 1 + n_head - 1)
+            for d in range(1, n_key):
+                c = pltpu.make_async_remote_copy(
+                    src_ref=img.at[it, key, at],
+                    dst_ref=img.at[it, key, at],
+                    send_sem=img_ss.at[it, d, g],
+                    recv_sem=img_rs.at[it, d, g],
+                    device_id={"key": lax.rem(key + d, n_key)},
+                    device_id_type=MESH,
+                )
+                c.start()
+                copies.append(c)
         if it == 0:
-            pl.semaphore_wait(barrier, n_key - 1 + n_head - 1)
-        copies = []
-        for d in range(1, n_key):
-            c = pltpu.make_async_remote_copy(
-                src_ref=img.at[it, key],
-                dst_ref=img.at[it, key],
-                send_sem=img_ss.at[it, d],
-                recv_sem=img_rs.at[it, d],
-                device_id={"key": lax.rem(key + d, n_key)},
-                device_id_type=MESH,
-            )
-            c.start()
-            copies.append(c)
+            for c in vs_in + [w_in]:
+                c.start()
         dots = dot_nt(dir_b, keys_b)
         bref[...] = dot_high(mix * dots, keys) + ridge * dref[...]
         for c in copies:
             c.wait_recv()
         sends += copies
-        applied = jnp.concatenate([img[it, j] for j in range(n_key)], axis=1) + bref[...]
+        applied = jnp.concatenate([img[it, j].astype(F32) for j in range(n_key)], axis=1) + bref[...]
         direction = dref[...]
         step = sq_norm / jnp.sum(direction * applied, axis=1, keepdims=True)
         if it == 0:
@@ -216,7 +220,7 @@
         sq_norm = new_norm
 
     dir_b = dref[...].astype(BF16)
-    image = local_product(dir_b, False)
+    image = jnp.concatenate([group_product(dir_b, g, False) for g in range(groups)], axis=0)
     den_send[...] = as_row(jnp.sum(image * dref[:, mine], axis=1, keepdims=True))
     for d in range(1, n_key):
         c = pltpu.make_async_remote_copy(
@@ -233,7 +237,8 @@
 
     x_rows = xref[:, mine].astype(BF16)
     d_rows = dref[:, mine].astype(BF16)
-    for g in range(n // GROUP):
+    reads = []
+    for g in range(groups):
         at = slice(g * GROUP, (g + 1) * GROUP)
         lhs = jnp.concatenate([x_rows[at], d_rows[at]], axis=0)
         acc_x = acc_d = None
@@ -248,21 +253,20 @@
         acc_d = (decay[at] * acc_d).astype(BF16)
         for j in range(n_key):
             cols = slice(j * vcols, (j + 1) * vcols)
-            rd_send[j, 0, at, :] = acc_x[:, cols]
-            rd_send[j, 1, at, :] = acc_d[:, cols]
-    reads = []
-    for d in range(1, n_key):
-        to = lax.rem(key + d, n_key)
-        c = pltpu.make_async_remote_copy(
-            src_ref=rd_send.at[to],
-            dst_ref=rd_recv.at[d],
-            send_sem=rd_ss.at[d],
-            recv_sem=rd_rs.at[d],
-            device_id={"key": to},
-            device_id_type=MESH,
-        )
-        c.start()
-        reads.append(c)
+            rd_send[g, j, 0] = acc_x[:, cols]
+            rd_send[g, j, 1] = acc_d[:, cols]
+        for d in range(1, n_key):
+            to = lax.rem(key + d, n_key)
+            c = pltpu.make_async_remote_copy(
+                src_ref=rd_send.at[g, to],
+                dst_ref=rd_recv.at[g, d],
+                send_sem=rd_ss.at[g, d],
+                recv_sem=rd_rs.at[g, d],
+                device_id={"key": to},
+                device_id_type=MESH,
+            )
+            c.start()
+            reads.append(c)
     sends += reads
     dots_d = dot_nt(dir_b, keys_b)
     dots_x = dot_nt(xref[...].astype(BF16), keys_b)
@@ -270,16 +274,21 @@
     den = jnp.sum(base * dref[...], axis=1, keepdims=True) + as_column(den_send[...])
     vcol = pl.ds(pl.multiple_of(key * vcols, 128), vcols)
     vals = vf[:, vcol]
-    read_x = dot_high(mix * dots_x, vals) + rd_send[key, 0].astype(F32)
-    read_d = dot_high(mix * dots_d, vals) + rd_send[key, 1].astype(F32)
+
+    def stacked(ref, slot, part):
+        return jnp.concatenate([ref[g, slot, part].astype(F32) for g in range(groups)], axis=0)
+
+    read_x = dot_high(mix * dots_x, vals) + stacked(rd_send, key, 0)
+    read_d = dot_high(mix * dots_d, vals) + stacked(rd_send, key, 1)
     for d in range(1, n_key):
         dens[d - 1].wait_recv()
         den = den + as_column(den_recv[d])
     step = sq_norm / den
+    for c in reads:
+        c.wait_recv()
     for d in range(1, n_key):
-        reads[d - 1].wait_recv()
-        read_x = read_x + rd_recv[d, 0].astype(F32)
-        read_d = read_d + rd_recv[d, 1].astype(F32)
+        read_x = read_x + stacked(rd_recv, d, 0)
+        read_d = read_d + stacked(rd_recv, d, 1)
     read = read_x + step * read_d
 
     sq_send[...] = as_row(jnp.sum(read * read, axis=1, keepdims=True))
@@ -423,9 +432,9 @@
                 pltpu.VMEM((n, width), F32),
                 pltpu.VMEM((n, width), F32),
                 pltpu.VMEM((n, width), F32),
-                pltpu.VMEM((ITERS - 1, n_key, n, rows), F32),
-                pltpu.VMEM((n_key, 2, n, vcols), BF16),
-                pltpu.VMEM((n_key, 2, n, vcols), BF16),
+                pltpu.VMEM((ITERS - 1, n_key, n, rows), BF16),
+                pltpu.VMEM((n // GROUP, n_key, 2, GROUP, vcols), BF16),
+                pltpu.VMEM((n // GROUP, n_key, 2, GROUP, vcols), BF16),
                 pltpu.VMEM((8, 128), F32),
                 pltpu.VMEM((n_key, 8, 128), F32),
                 pltpu.VMEM((8, 128), F32),
@@ -442,10 +451,10 @@
                 dma((seqs,)),
                 dma((seqs,)),
                 dma,
-                dma((ITERS - 1, n_key)),
-                dma((ITERS - 1, n_key)),
-                dma((n_key,)),
-                dma((n_key,)),
+                dma((ITERS - 1, n_key, n // GROUP)),
+                dma((ITERS - 1, n_key, n // GROUP)),
+                dma((n // GROUP, n_key)),
+                dma((n // GROUP, n_key)),
                 dma((n_key,)),
                 dma((n_key,)),
                 dma((n_key,)),

time: 37.4 us -> 35.4 us (0.947)
  Pallas kernels: 35.1 us -> 33.2 us
    pallas_call x1, Pallas kernels: 35.1 us -> 33.2 us  [body(): pl.pallas_call(functools.partial(kernel, n_key, n_head), out_shape=jax.Sh...]
where the time goes in v3:
time: 35.4 us; the launch traced here: 35.2 us
  Pallas kernels  33.2 us (94%)
  local copies, waits for them, and re-layouts  1.39 us (4%)
  between operations  0.66 us (2%)
    pallas_call x1, Pallas kernels, body(): pl.pallas_call(functools.partial(kernel, n_key, n_head), out_shape=jax.Sh...  33.2 us
    unnamed x1, local copies, waits for them, and re-layouts  1.39 us

profile of v3, /device:TPU:0, one launch (start us, length us, event | category | flops | bytes accessed | tf_op | source)
XLA Modules:
  0.0 35.2 jit_solution(17816213497843842440)
XLA Ops:
  0.7 33.2 %shard_map.100 = bf16[8,4,512]{2,1,0:T(4,128)(2,1)} custom-call(bf16[8,1,4,1024]{3,2,1,0:T(4,128)(2,1)} %q_h.1, bf16[8,1,4,1024]{3,2,1,0:T(4,128)(2,1)} %k_h.1, bf16[8,1,4,1024]{3,2,1,0:T(4,128)(2,1)} %v_h.1, f32[1,4,8]{2,1,0:T(4,128)} %bitcast.2, f32[1,4,8]{2,1,0:T(4,128)} %bitcast.3, f32[1]{0:T(128)S(6)} %copy.12.ridge_ref, f32[1,256]{1,0:T(1,128)} %gain_h.1, ...), custom_call_target="tpu_custom_call" | custom-call | tf_op jit(solution)/shard_map/pallas_call | solution.py:412
  33.8 1.4 %copy.13 = bf16[8,4,512]{2,1,0:T(4,128)(2,1)} copy(bf16[8,4,512]{2,1,0:T(4,128)(2,1)} %shard_map.100) | data formatting | bytes 65536

commit v4 on v3

--- a/solution.py
+++ b/solution.py
@@ -220,21 +220,6 @@
         sq_norm = new_norm
 
     dir_b = dref[...].astype(BF16)
-    image = jnp.concatenate([group_product(dir_b, g, False) for g in range(groups)], axis=0)
-    den_send[...] = as_row(jnp.sum(image * dref[:, mine], axis=1, keepdims=True))
-    for d in range(1, n_key):
-        c = pltpu.make_async_remote_copy(
-            src_ref=den_send,
-            dst_ref=den_recv.at[d],
-            send_sem=den_ss.at[d],
-            recv_sem=den_rs.at[d],
-            device_id={"key": lax.rem(key + d, n_key)},
-            device_id_type=MESH,
-        )
-        c.start()
-        sends.append(c)
-    dens = sends[-(n_key - 1) :]
-
     x_rows = xref[:, mine].astype(BF16)
     d_rows = dref[:, mine].astype(BF16)
     reads = []
@@ -268,6 +253,21 @@
             c.start()
             reads.append(c)
     sends += reads
+    image = jnp.concatenate([group_product(dir_b, g, False) for g in range(groups)], axis=0)
+    den_send[...] = as_row(jnp.sum(image * dref[:, mine], axis=1, keepdims=True))
+    for d in range(1, n_key):
+        c = pltpu.make_async_remote_copy(
+            src_ref=den_send,
+            dst_ref=den_recv.at[d],
+            send_sem=den_ss.at[d],
+            recv_sem=den_rs.at[d],
+            device_id={"key": lax.rem(key + d, n_key)},
+            device_id_type=MESH,
+        )
+        c.start()
+        sends.append(c)
+    dens = sends[-(n_key - 1) :]
+
     dots_d = dot_nt(dir_b, keys_b)
     dots_x = dot_nt(xref[...].astype(BF16), keys_b)
     base = dot_high(mix * dots_d, keys) + ridge * dref[...]
@@ -317,31 +317,31 @@
         at = pl.multiple_of((to_key * n_head + to_head) * block, 128)
         return jnp.dot(gained, w_v[:, pl.ds(at, block)], preferred_element_type=F32)
 
-    order = list(range(1, n_head)) + [0]
+    order = sorted(range(1, n_head), key=lambda o: abs(2 * o - n_head)) + [0]
     core_copy, x_copy, z_copy = {}, {}, {}
     scale = []
 
     def stage_a(o):
         to = lax.rem(head + o, n_head)
-        for half in range(2):
-            core_send[o, half] = project(2 * half + 1 - core, to).astype(BF16)
-        c = pltpu.make_async_remote_copy(
-            src_ref=core_send.at[o],
-            dst_ref=core_recv.at[o],
-            send_sem=core_ss.at[o],
-            recv_sem=core_rs.at[o],
-            device_id={"key": partner},
-            device_id_type=MESH,
-        )
-        c.start()
-        core_copy[o] = c
-        for half in range(2):
-            own[o, half] = project(2 * half + core, to)
+        core_copy[o] = []
+        for part, side in enumerate((1 - chip, chip)):
+            core_send[o, part] = project(2 * side + 1 - core, to).astype(BF16)
+            c = pltpu.make_async_remote_copy(
+                src_ref=core_send.at[o, part],
+                dst_ref=core_recv.at[o, part],
+                send_sem=core_ss.at[o, part],
+                recv_sem=core_rs.at[o, part],
+                device_id={"key": partner},
+                device_id_type=MESH,
+            )
+            c.start()
+            core_copy[o].append(c)
+        for part, side in enumerate((1 - chip, chip)):
+            own[o, part] = project(2 * side + core, to)
 
     def stage_b(o):
-        core_copy[o].wait_recv()
-        other = 1 - chip
-        x_send[o] = (own[o, other] + core_recv[o, other].astype(F32)).astype(BF16)
+        core_copy[o][0].wait_recv()
+        x_send[o] = (own[o, 0] + core_recv[o, 0].astype(F32)).astype(BF16)
         c = pltpu.make_async_remote_copy(
             src_ref=x_send.at[o],
             dst_ref=x_recv.at[o],
@@ -352,7 +352,8 @@
         )
         c.start()
         x_copy[o] = c
-        keep[o] = own[o, chip] + core_recv[o, chip].astype(F32)
+        core_copy[o][1].wait_recv()
+        keep[o] = own[o, 1] + core_recv[o, 1].astype(F32)
 
     def stage_c(o):
         if not scale:
@@ -392,7 +393,7 @@
     keep[0] = result
     for s in range(seqs):
         out_ref[s] = keep[0, s * draft : (s + 1) * draft, :].astype(BF16)
-    for c in sends + list(core_copy.values()) + list(x_copy.values()) + list(z_copy.values()):
+    for c in sends + [c for pair in core_copy.values() for c in pair] + list(x_copy.values()) + list(z_copy.values()):
         c.wait_send()
 
 
@@ -459,8 +460,8 @@
                 dma((n_key,)),
                 dma((n_key,)),
                 dma((n_key,)),
-                dma((n_head,)),
-                dma((n_head,)),
+                dma((n_head, 2)),
+                dma((n_head, 2)),
                 dma((n_head,)),
                 dma((n_head,)),
                 dma((n_head,)),

time: 35.4 us -> 35.6 us (level)
  no operation moved by 1% of the time
where the time goes in v4:
time: 35.6 us; the launch traced here: 35.4 us
  Pallas kernels  33.3 us (94%)
  local copies, waits for them, and re-layouts  1.39 us (4%)
  between operations  0.66 us (2%)
    pallas_call x1, Pallas kernels, body(): pl.pallas_call(functools.partial(kernel, n_key, n_head), out_shape=jax.Sh...  33.3 us
    unnamed x1, local copies, waits for them, and re-layouts  1.39 us

profile of v4, /device:TPU:0, one launch (start us, length us, event | category | flops | bytes accessed | tf_op | source)
XLA Modules:
  0.0 35.4 jit_solution(16137031229753310107)
XLA Ops:
  0.7 33.3 %shard_map.100 = bf16[8,4,512]{2,1,0:T(4,128)(2,1)} custom-call(bf16[8,1,4,1024]{3,2,1,0:T(4,128)(2,1)} %q_h.1, bf16[8,1,4,1024]{3,2,1,0:T(4,128)(2,1)} %k_h.1, bf16[8,1,4,1024]{3,2,1,0:T(4,128)(2,1)} %v_h.1, f32[1,4,8]{2,1,0:T(4,128)} %bitcast.2, f32[1,4,8]{2,1,0:T(4,128)} %bitcast.3, f32[1]{0:T(128)S(6)} %copy.12.ridge_ref, f32[1,256]{1,0:T(1,128)} %gain_h.1, ...), custom_call_target="tpu_custom_call" | custom-call | tf_op jit(solution)/shard_map/pallas_call | solution.py:413
  34.0 1.4 %copy.13 = bf16[8,4,512]{2,1,0:T(4,128)(2,1)} copy(bf16[8,4,512]{2,1,0:T(4,128)(2,1)} %shard_map.100) | data formatting | bytes 65536

commit v5 on v4

--- a/solution.py
+++ b/solution.py
@@ -11,7 +11,6 @@
 MESH = pl.DeviceIdType.MESH
 F32 = jnp.float32
 BF16 = jnp.bfloat16
-HIGH = lax.Precision.HIGHEST
 GROUP = 16
 
 
@@ -19,10 +18,16 @@
     return lax.dot_general(a, b, (((1,), (1,)), ((), ())), preferred_element_type=F32)
 
 
-def dot_high(a, b):
-    return lax.dot_general(
-        a, b, (((1,), (0,)), ((), ())), precision=HIGH, preferred_element_type=F32
+def dot_split(a, b):
+    top = a.astype(BF16)
+    rest = a - top.astype(F32)
+    middle = rest.astype(BF16)
+    low = (rest - middle.astype(F32)).astype(BF16)
+    m = a.shape[0]
+    parts = jnp.dot(
+        jnp.concatenate([top, middle, low], axis=0), b, preferred_element_type=F32
     )
+    return parts[:m] + (parts[m : 2 * m] + parts[2 * m :])
 
 
 def kernel(
@@ -202,7 +207,7 @@
             for c in vs_in + [w_in]:
                 c.start()
         dots = dot_nt(dir_b, keys_b)
-        bref[...] = dot_high(mix * dots, keys) + ridge * dref[...]
+        bref[...] = dot_split(mix * dots, keys_b) + ridge * dref[...]
         for c in copies:
             c.wait_recv()
         sends += copies
@@ -270,16 +275,16 @@
 
     dots_d = dot_nt(dir_b, keys_b)
     dots_x = dot_nt(xref[...].astype(BF16), keys_b)
-    base = dot_high(mix * dots_d, keys) + ridge * dref[...]
+    base = dot_split(mix * dots_d, keys_b) + ridge * dref[...]
     den = jnp.sum(base * dref[...], axis=1, keepdims=True) + as_column(den_send[...])
     vcol = pl.ds(pl.multiple_of(key * vcols, 128), vcols)
-    vals = vf[:, vcol]
+    vals = vf[:, vcol].astype(BF16)
 
     def stacked(ref, slot, part):
         return jnp.concatenate([ref[g, slot, part].astype(F32) for g in range(groups)], axis=0)
 
-    read_x = dot_high(mix * dots_x, vals) + stacked(rd_send, key, 0)
-    read_d = dot_high(mix * dots_d, vals) + stacked(rd_send, key, 1)
+    read_x = dot_split(mix * dots_x, vals) + stacked(rd_send, key, 0)
+    read_d = dot_split(mix * dots_d, vals) + stacked(rd_send, key, 1)
     for d in range(1, n_key):
         dens[d - 1].wait_recv()
         den = den + as_column(den_recv[d])

time: 35.6 us -> 35.5 us (level)
  no operation moved by 1% of the time
where the time goes in v5:
time: 35.5 us; the launch traced here: 35.3 us
  Pallas kernels  33.3 us (94%)
  local copies, waits for them, and re-layouts  1.39 us (4%)
  between operations  0.66 us (2%)
    pallas_call x1, Pallas kernels, body(): pl.pallas_call(functools.partial(kernel, n_key, n_head), out_shape=jax.Sh...  33.3 us
    unnamed x1, local copies, waits for them, and re-layouts  1.39 us

profile of v5, /device:TPU:0, one launch (start us, length us, event | category | flops | bytes accessed | tf_op | source)
XLA Modules:
  0.0 35.3 jit_solution(5527471051558712985)
XLA Ops:
  0.7 33.3 %shard_map.100 = bf16[8,4,512]{2,1,0:T(4,128)(2,1)} custom-call(bf16[8,1,4,1024]{3,2,1,0:T(4,128)(2,1)} %q_h.1, bf16[8,1,4,1024]{3,2,1,0:T(4,128)(2,1)} %k_h.1, bf16[8,1,4,1024]{3,2,1,0:T(4,128)(2,1)} %v_h.1, f32[1,4,8]{2,1,0:T(4,128)} %bitcast.2, f32[1,4,8]{2,1,0:T(4,128)} %bitcast.3, f32[1]{0:T(128)S(6)} %copy.12.ridge_ref, f32[1,256]{1,0:T(1,128)} %gain_h.1, ...), custom_call_target="tpu_custom_call" | custom-call | tf_op jit(solution)/shard_map/pallas_call | solution.py:418
  33.9 1.4 %copy.13 = bf16[8,4,512]{2,1,0:T(4,128)(2,1)} copy(bf16[8,4,512]{2,1,0:T(4,128)(2,1)} %shard_map.100) | data formatting | bytes 65536
